TPU v7x, 256 devices: a whole 4x4x8 slice. The times are simulated.
256 devices in a mesh: seq: 32 (over y, z), head: 8 (over x, core).
Axes of the slice: x: 4, y: 4, z: 8, core: 2. Of those that a mesh axis runs over, the one named last changes fastest.
Arguments:
- block_input: bfloat16 [4096, 3072], P('seq'), may hold values from -12 to 12
- grad_output: bfloat16 [4096, 3072], P('seq'), may hold values from -6 to 6
- weights: bfloat16 [3072, 4, 3072], P('seq', None, 'head'), may hold values from -0.109375 to 0.109375
- clip_ids: int32 [32], replicated, may hold values from 0 to 2, never falling along the last dimension, each value on 1 to 16 neighbouring positions
Outputs:
- grad_input: bfloat16 [4096, 3072], P('seq', 'head')
- grad_weights: bfloat16 [3072, 4, 3072], P('seq', None, 'head')
Inputs may be any that keep to these rules, and one draw needn't show every extreme that they name: `clip_ids`: clip numbers never fall from one frame to the next; every clip number of 0 to 2 is used, each clip spans 1 to 16 frames and one spans exactly 16.
All inputs are finite; a program needn't handle non-finite values.
Results may differ from a plain program's by a relative error of at most 0.018.
Values may be sent and summed in bfloat16 or wider, within the bound.
No kernel may reach another device: no remote copies, remote signals or barrier semaphores. Data moves between devices by JAX's collectives and lax.ppermute only.
A program may use at most 128 MiB of HBM per device.

v0:
```python
import jax
import jax.numpy as jnp
from jax import lax
from jax.sharding import Mesh
from jax.sharding import PartitionSpec as P

HD = 128
WIN = 1
P_SIZE = 128
SEQ = ("seq_0", "seq_1")
big_negative = -1e30


def padded(cells, sides, width):
    for axis, dim in sides:
        count = lax.axis_size(axis)
        ends = count - 1
        head = lax.slice_in_dim(cells, 0, width, axis=dim)
        tail = lax.slice_in_dim(cells, cells.shape[dim] - width, cells.shape[dim], axis=dim)
        cells = jnp.concatenate(
            [
                lax.ppermute(tail, axis, [(i, (i + 1) % count) for i in range(ends)]),
                cells,
                lax.ppermute(head, axis, [((i + 1) % count, i) for i in range(ends)]),
            ],
            axis=dim,
        )
    return cells


def split_up(x, dim, count):
    before, after = (x.shape[:dim], x.shape[dim + 1 :])
    return jnp.moveaxis(x.reshape(*before, count, -1, *after), dim, 0)


def piece_ends(length, count):
    unit = 8 if length >= 8 * count else 1
    return [length // unit * k // count * unit for k in range(1, count)]


def own_block(pieces, axes, sequence):
    inside = pieces.shape[1:]
    pieces = pieces.reshape(*(lax.axis_size(a) for a in axes), *inside)
    pieces = jnp.moveaxis(pieces, sequence, range(len(axes))).reshape(-1, *inside)
    for k in sequence:
        pieces = lax.psum_scatter(pieces, axes[k], scatter_dimension=0, tiled=True)
    return pieces[0]


def spread_scatter(x, axes, dim):
    pieces = split_up(x, dim, lax.axis_size(axes))
    widest = max(range(1, max(2, pieces.ndim - 1)), key=lambda d: pieces.shape[d])
    count, outs = (len(axes), [])
    for first, section in enumerate(
        jnp.split(pieces, piece_ends(pieces.shape[widest], count), axis=widest)
    ):
        if section.size:
            sequence = [(first + k) % count for k in range(count)]
            outs.append(own_block(section, axes, sequence))
    return jnp.concatenate(outs, axis=widest - 1)


def sent_and_summed(x, axis, dim):
    pieces = split_up(x, dim, lax.axis_size(axis))
    arrived = lax.all_to_all(pieces, axis, split_axis=0, concat_axis=0, tiled=True)
    return arrived.astype(jnp.float32).sum(axis=0)


def attend(query_rows, key_ext, value_ext, grad_rows, clip_ext):
    frame_count = clip_ext.shape[0] - 2 * WIN
    window_len = 2 * WIN + 1
    head_count = query_rows.shape[1] // HD
    score_scale = HD ** (-0.5)
    query_frames = query_rows.reshape(frame_count, P_SIZE, head_count, HD)
    key_frames = key_ext.reshape(frame_count + 2 * WIN, P_SIZE, head_count, HD)
    value_frames = value_ext.reshape(frame_count + 2 * WIN, P_SIZE, head_count, HD)
    grad_frames = grad_rows.reshape(frame_count, P_SIZE, head_count, HD)
    key_window = jnp.stack(
        [key_frames[offset : offset + frame_count] for offset in range(window_len)], axis=1
    )
    value_window = jnp.stack(
        [value_frames[offset : offset + frame_count] for offset in range(window_len)], axis=1
    )
    clip_window = jnp.stack(
        [clip_ext[offset : offset + frame_count] for offset in range(window_len)], axis=1
    )
    allowed = clip_window == clip_ext[WIN : WIN + frame_count][:, None]
    allowed = allowed[:, None, None, :, None]
    scores = (
        jnp.einsum(
            "fihc,fojhc->fhioj", query_frames, key_window, preferred_element_type=jnp.float32
        )
        * score_scale
    )
    masked = jnp.where(allowed, scores, big_negative)
    top_score = jnp.max(masked, axis=(3, 4), keepdims=True)
    expo_terms = jnp.where(allowed, jnp.exp(masked - top_score), 0.0)
    attn_prob = expo_terms / jnp.sum(expo_terms, axis=(3, 4), keepdims=True)
    prob_low = attn_prob.astype(jnp.bfloat16)
    attn_out = jnp.einsum(
        "fhioj,fojhc->fihc", prob_low, value_window, preferred_element_type=jnp.float32
    )
    delta_row = jnp.sum(grad_frames.astype(jnp.float32) * attn_out, axis=3)
    delta_row = jnp.transpose(delta_row, (0, 2, 1))[:, :, :, None, None]
    grad_prob = jnp.einsum(
        "fihc,fojhc->fhioj", grad_frames, value_window, preferred_element_type=jnp.float32
    )
    grad_score = (attn_prob * (grad_prob - delta_row)).astype(jnp.bfloat16)
    grad_query = (
        jnp.einsum("fhioj,fojhc->fihc", grad_score, key_window, preferred_element_type=jnp.float32)
        * score_scale
    )
    grad_key_window = (
        jnp.einsum(
            "fhioj,fihc->fojhc", grad_score, query_frames, preferred_element_type=jnp.float32
        )
        * score_scale
    )
    grad_value_window = jnp.einsum(
        "fhioj,fihc->fojhc", prob_low, grad_frames, preferred_element_type=jnp.float32
    )
    grad_key = jnp.zeros((frame_count + 2 * WIN, P_SIZE, head_count, HD), jnp.float32)
    grad_value = jnp.zeros((frame_count + 2 * WIN, P_SIZE, head_count, HD), jnp.float32)
    for offset in range(window_len):
        grad_key = grad_key.at[offset : offset + frame_count].add(grad_key_window[:, offset])
        grad_value = grad_value.at[offset : offset + frame_count].add(grad_value_window[:, offset])
    column_count = head_count * HD
    return (
        grad_query.reshape(frame_count * P_SIZE, column_count),
        grad_key.reshape((frame_count + 2 * WIN) * P_SIZE, column_count),
        grad_value.reshape((frame_count + 2 * WIN) * P_SIZE, column_count),
        attn_out.astype(jnp.bfloat16).reshape(frame_count * P_SIZE, column_count),
    )


def on_device(block_input, grad_output, weights, clip_ids):
    row_count = block_input.shape[0]
    feature_count = block_input.shape[1]
    slab_rows = weights.shape[0]
    column_count = weights.shape[2]
    frame_count = row_count // P_SIZE
    rim_rows = WIN * P_SIZE
    seq_index = lax.axis_index(SEQ)
    full_weights = lax.all_gather(weights, SEQ, axis=0, tiled=True)
    projected = jnp.dot(
        block_input,
        full_weights[:, :3].reshape(feature_count, 3 * column_count),
        preferred_element_type=jnp.float32,
    )
    grad_attn = jnp.dot(grad_output, full_weights[:, 3], preferred_element_type=jnp.float32)
    projected = projected.astype(jnp.bfloat16)
    grad_attn = grad_attn.astype(jnp.bfloat16)
    query_rows = projected[:, :column_count]
    key_value = jnp.stack(
        [projected[:, column_count : 2 * column_count], projected[:, 2 * column_count :]]
    )
    extended = padded(key_value, ((SEQ, 1),), rim_rows)
    clip_rim = jnp.full((WIN,), -1, jnp.int32)
    clip_padded = jnp.concatenate([clip_rim, clip_ids, clip_rim])
    clip_ext = lax.dynamic_slice_in_dim(
        clip_padded, seq_index * frame_count, frame_count + 2 * WIN, 0
    )
    grad_query, grad_key, grad_value, attn_low = attend(
        query_rows, extended[0], extended[1], grad_attn, clip_ext
    )
    grad_pair = jnp.stack([grad_key, grad_value])
    lower_rim = grad_pair[:, :rim_rows]
    upper_rim = grad_pair[:, rim_rows + row_count :]
    inner_rows = grad_pair[:, rim_rows : rim_rows + row_count]
    both_rims = jnp.concatenate([lower_rim, upper_rim], axis=1)
    beside_all = padded(both_rims, ((SEQ, 1),), rim_rows)
    from_below = beside_all[:, :rim_rows]
    from_above = beside_all[:, 3 * rim_rows :]
    inner_rows = inner_rows.at[:, :rim_rows].add(from_below)
    inner_rows = inner_rows.at[:, row_count - rim_rows :].add(from_above)
    grad_qkv = jnp.concatenate([grad_query, inner_rows[0], inner_rows[1]], axis=1).astype(
        jnp.bfloat16
    )
    grad_weights = (
        spread_scatter(
            jnp.concatenate(
                [
                    lax.dot_general(
                        block_input,
                        grad_qkv,
                        (((0,), (0,)), ((), ())),
                        preferred_element_type=jnp.float32,
                    ).reshape(slab_rows * lax.axis_size(SEQ), 3, column_count),
                    lax.dot_general(
                        grad_output,
                        attn_low,
                        (((0,), (0,)), ((), ())),
                        preferred_element_type=jnp.float32,
                    )[:, None, :],
                ],
                axis=1,
            ).astype(jnp.bfloat16),
            SEQ,
            0,
        )
        .astype(jnp.float32)
        .astype(jnp.bfloat16)
    )
    partial_input = lax.dot_general(
        grad_qkv,
        full_weights[:, :3].reshape(feature_count, 3 * column_count),
        (((1,), (1,)), ((), ())),
        preferred_element_type=jnp.float32,
    )
    grad_input = sent_and_summed(partial_input.astype(jnp.bfloat16), "head", 1).astype(jnp.bfloat16)
    return (grad_input, grad_weights)


def solution(mesh):
    torus = Mesh(mesh.devices.reshape(4, 8, mesh.shape["head"]), ("seq_0", "seq_1", "head"))
    return jax.shard_map(
        on_device,
        mesh=torus,
        in_specs=(P(SEQ, None), P(SEQ, None), P(SEQ, None, "head"), P()),
        out_specs=(P(SEQ, "head"), P(SEQ, None, "head")),
        check_vma=False,
    )
```

profile of v0, /device:TPU:2, one launch (start us, length us, event | category | flops | bytes accessed | tf_op | source)
XLA Modules:
  0.0 428.7 jit_solution(6999756514082008056)
XLA Ops:
  8.0 0.7 pad_add_fusion
  10.1 106.7 %all-gather.2.cloned.1.call-done = bf16[3072,4,384]{2,1,0:T(4,128)(2,1)} async-done(((bf16[96,4,384]{2,1,0:T(4,128)(2,1)}), bf16[3072,4,384]{2,1,0:T(4,128)(2,1)}) %all-gather.2.cloned.1.call-update) | async-done | bytes 9437200 | tf_op jit(solution)/shard_map/all_gather | solution.py:144
  116.7 14.5 %copy.165 = bf16[3072,3,384]{0,2,1:T(8,128)(2,1)} copy(bf16[3072,3,384]{2,1,0:T(4,128)(2,1)} %bitcast.151) | data formatting | bytes 14155776
  131.2 5.3 %convolution_convert_fusion.3 = bf16[128,1152]{1,0:T(8,128)(2,1)S(1)} fusion(bf16[128,3072]{1,0:T(8,128)(2,1)S(1)} %copy-done, bf16[3072,1152]{0,1:T(8,128)(2,1)} %bitcast.149), kind=kOutput, calls=%fused_computation.8 | convolution fusion | flops 906117120 | bytes 8159232 | tf_op jit(solution)/shard_map/dot_general | solution.py:145
  136.7 1.4 collective-permute-start.1
  138.1 6.8 %slice.323 = bf16[3072,1,384]{2,1,0:T(2,128)(2,1)S(1)} slice(bf16[3072,4,384]{2,1,0:T(4,128)(2,1)} %all-gather.2.cloned.1.call-done), slice={[0:3072], [3:4], [0:384]} | slice | bytes 4718592 | tf_op jit(solution)/shard_map/slice | solution.py:150
  145.7 4.6 %collective-permute-start = (bf16[2,128,384]{2,1,0:T(8,128)(2,1)S(1)}, bf16[2,128,384]{2,1,0:T(8,128)(2,1)S(1)}, u32[]{:S(2)}, u32[]{:S(2)}) collective-permute-start(bf16[2,128,384]{2,1,0:T(8,128)(2,1)S(1)} %pad_maximum_fusion.4), channel_id=1, source_target_pairs={{0,8},{8,16},{16,24},{24,32},{32,40},{40,48},{48,56},{56,64},{64,7... | collective-permute-start | bytes 589832 | tf_op jit(solution)/shard_map/ppermute | solution.py:22
  151.5 1.9 collective-permute-done
  155.0 1.0 fusion.32
  158.8 1.0 copy-done.2
  159.8 1.0 fusion.30
  160.8 5.1 %collective-permute-start.2 = (f32[2,128,384]{2,1,0:T(8,128)}, f32[2,128,384]{2,1,0:T(8,128)}, u32[]{:S(2)}, u32[]{:S(2)}) collective-permute-start(f32[2,128,384]{2,1,0:T(8,128)} %get-tuple-element.122), channel_id=1, source_target_pairs={{0,8},{8,16},{16,24},{24,32},{32,40},{40,48},{48,56},{56,64},{64,7... | collective-permute-start | bytes 1179656 | tf_op jit(solution)/shard_map/ppermute | solution.py:22
  165.9 1.5 collective-permute-start.3
  167.4 1.4 fusion.8
  168.9 2.0 fusion.2
  170.9 2.4 copy.144
  173.3 4.9 %copy.145 = bf16[32,96,1,384]{1,0,3,2:T(8,128)(2,1)} copy(bf16[32,96,1,384]{3,1,0,2:T(8,128)(2,1)} %bitcast.153) | data formatting | bytes 4718592 | tf_op jit(solution)/shard_map/concatenate | solution.py:181
  178.3 1.3 fusion.14
  179.6 4.9 %fusion.1 = bf16[3072,1152]{0,1:T(8,128)(2,1)} fusion(bf16[128,3072]{1,0:T(8,128)(2,1)S(1)} %copy-done, bf16[128,384]{1,0:T(8,128)(2,1)S(1)} %get-tuple-element.132, bf16[128,384]{1,0:T(8,128)(2,1)S(1)} %get-tuple-element.131, bf16[128,384]{1,0:T(8,128)(2,1)S(1)} %copy.142), kind=kOutput, calls=%fused_computation.4 | convolution fusion | flops 910393344 | bytes 8159232 | tf_op jit(solution)/shard_map/dot_general | solution.py:183
  184.5 15.7 %concatenate.45 = bf16[32,96,3,384]{1,0,3,2:T(8,128)(2,1)} reshape(bf16[3072,1152]{0,1:T(8,128)(2,1)} %fusion.1) | data formatting | bytes 14155776 | tf_op jit(solution)/shard_map/concatenate | solution.py:181
  200.2 20.5 %slice_maximum_fusion = (bf16[32,48,4,384]{1,0,3,2:T(8,128)(2,1)}, bf16[8,4,48,4,384]{2,0,1,4,3:T(8,128)(2,1)}) fusion(bf16[32,96,1,384]{1,0,3,2:T(8,128)(2,1)} %copy.145, bf16[32,96,3,384]{1,0,3,2:T(8,128)(2,1)} %concatenate.45), kind=kLoop, calls=%fused_computation.2 | loop fusion | flops 18874368 | bytes 18874368 | tf_op jit(solution)/shard_map/concatenate | solution.py:181
  220.7 14.1 %copy.147 = bf16[8,4,48,4,384]{4,2,3,1,0:T(8,128)(2,1)} copy(bf16[8,4,48,4,384]{2,0,1,4,3:T(8,128)(2,1)} %get-tuple-element.121) | data formatting | bytes 9437184 | tf_op jit(solution)/shard_map/transpose | solution.py:44
  234.8 14.1 %copy.146 = bf16[32,48,4,384]{3,1,2,0:T(8,128)(2,1)} copy(bf16[32,48,4,384]{1,0,3,2:T(8,128)(2,1)} %get-tuple-element.120) | data formatting | bytes 9437184 | tf_op jit(solution)/shard_map/split | solution.py:55
  248.9 48.2 %reduce-scatter.9.cloned.1.call-done = bf16[4,48,4,384]{3,1,2,0:T(8,128)(2,1)} async-done(((bf16[32,48,4,384]{3,1,2,0:T(8,128)(2,1)}), bf16[4,48,4,384]{3,1,2,0:T(8,128)(2,1)}) %reduce-scatter.9.cloned.1.call-update) | async-done | bytes 589840 | tf_op jit(solution)/shard_map/reduce_scatter | solution.py:46
  297.2 54.8 %reduce-scatter.5.cloned.1.call-done = bf16[8,48,4,384]{3,1,2,0:T(8,128)(2,1)} async-done(((bf16[32,48,4,384]{3,1,2,0:T(8,128)(2,1)}), bf16[8,48,4,384]{3,1,2,0:T(8,128)(2,1)}) %reduce-scatter.5.cloned.1.call-update) | async-done | bytes 1179664 | tf_op jit(solution)/shard_map/reduce_scatter | solution.py:46
  352.1 4.3 convolution_convert_fusion.2
  356.5 16.3 %all_to_all.5 = bf16[8,128,384]{2,1,0:T(8,128)(2,1)S(1)} all-to-all(bf16[8,128,384]{2,1,0:T(8,128)(2,1)S(1)} %bitcast.159), channel_id=1, replica_groups=mesh['seq_0'=4,'seq_1'=8,'head'=8] {'head'}, dimensions={0} | all-to-all | bytes 1572864 | tf_op jit(solution)/shard_map/all_to_all | solution.py:65
  372.8 0.8 reduce_sum.35
  373.6 5.1 %reduce-scatter.11.cloned.1.call-done = bf16[1,48,4,384]{3,1,2,0:T(8,128)(2,1)} async-done(((bf16[4,48,4,384]{3,1,2,0:T(8,128)(2,1)}), bf16[1,48,4,384]{3,1,2,0:T(8,128)(2,1)}) %reduce-scatter.11.cloned.1.call-update) | async-done | bytes 147472 | tf_op jit(solution)/shard_map/reduce_scatter | solution.py:46
  378.6 41.6 %reduce-scatter.7.cloned.1.call-done = bf16[1,48,4,384]{3,1,2,0:T(8,128)(2,1)} async-done(((bf16[8,48,4,384]{3,1,2,0:T(8,128)(2,1)}), bf16[1,48,4,384]{3,1,2,0:T(8,128)(2,1)}) %reduce-scatter.7.cloned.1.call-update) | async-done | bytes 147472 | tf_op jit(solution)/shard_map/reduce_scatter | solution.py:46
  420.3 1.0 pad_maximum_fusion.3
  421.3 0.9 copy.148
  (75 shorter events, 8.7 us)
Async XLA Ops:
  7.2 124.1 %copy-start = (bf16[128,3072]{1,0:T(8,128)(2,1)S(1)}, bf16[128,3072]{1,0:T(8,128)(2,1)}, u32[]{:S(2)}) copy-start(bf16[128,3072]{1,0:T(8,128)(2,1)} %param.24) | copy-start | bytes 2359300
  7.2 109.6 %all-gather.2.cloned.1.call-start = ((), (), s32[]{:S(2)}) async-start(), calls=%async_computation.5 | async-start | bytes 9732096 | tf_op jit(solution)/shard_map/all_gather | solution.py:144
  7.9 289.2 %reduce-scatter.9.cloned.1.call-start = ((), (), s32[]{:S(2)}) async-start(), calls=%async_computation.8 | async-start | bytes 5308416 | tf_op jit(solution)/shard_map/reduce_scatter | solution.py:46
  136.6 8.3 %copy-start.3 = (bf16[128,3072]{1,0:T(8,128)(2,1)S(1)}, bf16[128,3072]{1,0:T(8,128)(2,1)}, u32[]{:S(2)}) copy-start(bf16[128,3072]{1,0:T(8,128)(2,1)} %param.25) | copy-start | bytes 2359300
  136.7 14.3 %collective-permute-start.1 = (bf16[2,128,384]{2,1,0:T(8,128)(2,1)S(1)}, bf16[2,128,384]{2,1,0:T(8,128)(2,1)S(1)}, u32[]{:S(2)}, u32[]{:S(2)}) collective-permute-start(bf16[2,128,384]{2,1,0:T(8,128)(2,1)S(1)} %pad_maximum_fusion.4), channel_id=1, source_target_pairs={{8,0},{16,8},{24,16},{32,24},{40,32},{48,40},{56,48},{64,56},{72,6... | collective-permute-start | bytes 589832 | tf_op jit(solution)/shard_map/ppermute | solution.py:24
  145.7 7.7 %collective-permute-start = (bf16[2,128,384]{2,1,0:T(8,128)(2,1)S(1)}, bf16[2,128,384]{2,1,0:T(8,128)(2,1)S(1)}, u32[]{:S(2)}, u32[]{:S(2)}) collective-permute-start(bf16[2,128,384]{2,1,0:T(8,128)(2,1)S(1)} %pad_maximum_fusion.4), channel_id=1, source_target_pairs={{0,8},{8,16},{16,24},{24,32},{32,40},{40,48},{48,56},{56,64},{64,7... | collective-permute-start | bytes 589832 | tf_op jit(solution)/shard_map/ppermute | solution.py:22
  150.6 5.8 %copy-start.4 = (bf16[1,1,128,3,128]{4,2,1,3,0:T(8,128)(2,1)}, bf16[1,1,128,3,128]{4,2,1,3,0:T(8,128)(2,1)S(1)}, u32[]{:S(2)}) copy-start(bf16[1,1,128,3,128]{4,2,1,3,0:T(8,128)(2,1)S(1)} %copy.114) | copy-start | bytes 294916
  151.3 5.2 %copy-start.5 = (bf16[1,1,128,3,128]{4,2,1,3,0:T(8,128)(2,1)}, bf16[1,1,128,3,128]{4,2,1,3,0:T(8,128)(2,1)S(1)}, u32[]{:S(2)}) copy-start(bf16[1,1,128,3,128]{4,2,1,3,0:T(8,128)(2,1)S(1)} %copy.115) | copy-start | bytes 294916
  153.7 2.7 copy-start.6
  156.4 0.7 copy-start.7
  158.8 1.0 copy-start.2
  160.8 17.5 %collective-permute-start.2 = (f32[2,128,384]{2,1,0:T(8,128)}, f32[2,128,384]{2,1,0:T(8,128)}, u32[]{:S(2)}, u32[]{:S(2)}) collective-permute-start(f32[2,128,384]{2,1,0:T(8,128)} %get-tuple-element.122), channel_id=1, source_target_pairs={{0,8},{8,16},{16,24},{24,32},{32,40},{40,48},{48,56},{56,64},{64,7... | collective-permute-start | bytes 1179656 | tf_op jit(solution)/shard_map/ppermute | solution.py:22
  165.9 12.4 %collective-permute-start.3 = (f32[2,128,384]{2,1,0:T(8,128)}, f32[2,128,384]{2,1,0:T(8,128)}, u32[]{:S(2)}, u32[]{:S(2)}) collective-permute-start(f32[2,128,384]{2,1,0:T(8,128)} %get-tuple-element.123), channel_id=1, source_target_pairs={{8,0},{16,8},{24,16},{32,24},{40,32},{48,40},{56,48},{64,56},{72,6... | collective-permute-start | bytes 1179656 | tf_op jit(solution)/shard_map/ppermute | solution.py:24
  234.7 117.3 %reduce-scatter.5.cloned.1.call-start = ((), (), s32[]{:S(2)}) async-start(), calls=%async_computation.6 | async-start | bytes 5898240 | tf_op jit(solution)/shard_map/reduce_scatter | solution.py:46
  248.9 129.7 %reduce-scatter.11.cloned.1.call-start = ((), (), s32[]{:S(2)}) async-start(), calls=%async_computation.9 | async-start | bytes 737280 | tf_op jit(solution)/shard_map/reduce_scatter | solution.py:46
  297.2 123.1 %reduce-scatter.7.cloned.1.call-start = ((), (), s32[]{:S(2)}) async-start(), calls=%async_computation.7 | async-start | bytes 1327104 | tf_op jit(solution)/shard_map/reduce_scatter | solution.py:46
  352.1 70.0 %copy-start.1 = (bf16[128,3072]{1,0:T(8,128)(2,1)S(1)}, bf16[128,3072]{1,0:T(8,128)(2,1)}, u32[]{:S(2)}) copy-start(bf16[128,3072]{1,0:T(8,128)(2,1)} %param.24) | copy-start | bytes 2359300
Sparse Core Ops, SparseCore 0:
  10.6 106.1 all-gather.1
  234.9 62.2 reduce-scatter.8
  299.7 52.3 reduce-scatter.4
  354.5 24.1 reduce-scatter.10
  381.0 39.1 reduce-scatter.6
where the time goes:
time: 431 us; the launch traced here: 429 us
  waiting for transfers between devices  259 us (60%)
  local copies, waits for them, and re-layouts  80.1 us (19%)
  other arithmetic  25.5 us (6%)
  matrix products  20.7 us (5%)
  blocking collectives  16.3 us (4%)
  between operations  14.2 us (3%)
  starting transfers between devices  12.8 us (3%)
    reduce_scatter x4, waiting for transfers between devices, own_block(): pieces = lax.psum_scatter(pieces, axes[k], scatter_dimension=0, tiled=True)  150 us
    all_gather x1, waiting for transfers between devices, on_device(): full_weights = lax.all_gather(weights, SEQ, axis=0, tiled=True)  107 us
    concatenate x2, local copies, waits for them, and re-layouts, on_device(): jnp.concatenate([lax.dot_general(block_input, grad_qkv, (((0,), (0,)), ((...  20.6 us
    concatenate x1, other arithmetic, on_device(): jnp.concatenate([lax.dot_general(block_input, grad_qkv, (((0,), (0,)), ((...  20.5 us
    unnamed x19, local copies, waits for them, and re-layouts  16.8 us
    all_to_all x1, blocking collectives, sent_and_summed(): lax.all_to_all(pieces, axis, split_axis=0, concat_axis=0, tiled=True)  16.3 us
    split x1, local copies, waits for them, and re-layouts, spread_scatter(): jnp.split(pieces, piece_ends(pieces.shape[widest], count), axis=widest)  14.1 us
    transpose x1, local copies, waits for them, and re-layouts, own_block(): jnp.moveaxis(pieces, sequence, range(len(axes))).reshape(-1, *inside)  14.1 us
  transfers between devices with their start and end apart: 9, of which 6 were waited for; matrix products, arithmetic and copies ran while one was open for 10% of the time, Pallas kernels for 0%

commit v1 on v0

--- a/solution.py
+++ b/solution.py
@@ -141,7 +141,10 @@
     frame_count = row_count // P_SIZE
     rim_rows = WIN * P_SIZE
     seq_index = lax.axis_index(SEQ)
-    full_weights = lax.all_gather(weights, SEQ, axis=0, tiled=True)
+    count_2 = lax.axis_size(SEQ)
+    shards = jnp.stack([weights for _ in range(count_2)])
+    shards = lax.all_to_all(shards, SEQ, split_axis=0, concat_axis=0)
+    full_weights = jnp.concatenate(shards, axis=0)
     projected = jnp.dot(
         block_input,
         full_weights[:, :3].reshape(feature_count, 3 * column_count),

time: 431 us -> 569 us (1.32)
  waiting for transfers between devices: 259 us -> 373 us
  starting transfers between devices: 12.8 us -> 26.4 us
  local copies, waits for them, and re-layouts: 80.1 us -> 90.3 us
    all_to_all x0 -> x1, waiting for transfers between devices: none -> 212 us  [on_device(): shards = lax.all_to_all(shards, SEQ, split_axis=0, concat_axis=0)]
    all_gather x1 -> x0, waiting for transfers between devices: 107 us -> none  [on_device(): full_weights = lax.all_gather(weights, SEQ, axis=0, tiled=True)]
    unnamed x19 -> x21, local copies, waits for them, and re-layouts: 16.8 us -> 3.39 us
    all_to_all x0 -> x1, starting transfers between devices: none -> 11.7 us  [on_device(): shards = lax.all_to_all(shards, SEQ, split_axis=0, concat_axis=0)]
    slice x1 -> x2, local copies, waits for them, and re-layouts: 6.76 us -> 16.8 us  [on_device(): full_weights[:, :3].reshape(feature_count, 3 * column_count)]
    all_to_all x0 -> x1, local copies, waits for them, and re-layouts: none -> 8.52 us  [on_device(): shards = lax.all_to_all(shards, SEQ, split_axis=0, concat_axis=0)]
    reduce_scatter x4, waiting for transfers between devices: 150 us -> 158 us  [own_block(): pieces = lax.psum_scatter(pieces, axes[k], scatter_dimension=0, tiled=True)]
  transfers between devices with their start and end apart: 9 -> 9, of which waited for: 6 -> 7; matrix products, arithmetic and copies ran while one was open for 10% -> 6% of each run, Pallas kernels for 0% -> 0%
where the time goes in v1:
time: 569 us; the launch traced here: 568 us
  waiting for transfers between devices  373 us (66%)
  local copies, waits for them, and re-layouts  90.3 us (16%)
  starting transfers between devices  26.4 us (5%)
  other arithmetic  24.8 us (4%)
  matrix products  22.5 us (4%)
  blocking collectives  16.3 us (3%)
  between operations  14.2 us (2%)
    all_to_all x1, waiting for transfers between devices, on_device(): shards = lax.all_to_all(shards, SEQ, split_axis=0, concat_axis=0)  212 us
    reduce_scatter x4, waiting for transfers between devices, own_block(): pieces = lax.psum_scatter(pieces, axes[k], scatter_dimension=0, tiled=True)  158 us
    concatenate x2, local copies, waits for them, and re-layouts, on_device(): jnp.concatenate([lax.dot_general(block_input, grad_qkv, (((0,), (0,)), ((...  20.6 us
    concatenate x1, other arithmetic, on_device(): jnp.concatenate([lax.dot_general(block_input, grad_qkv, (((0,), (0,)), ((...  20.5 us
    slice x2, local copies, waits for them, and re-layouts, on_device(): full_weights[:, :3].reshape(feature_count, 3 * column_count)  16.8 us
    all_to_all x1, blocking collectives, sent_and_summed(): lax.all_to_all(pieces, axis, split_axis=0, concat_axis=0, tiled=True)  16.3 us
    split x1, local copies, waits for them, and re-layouts, spread_scatter(): jnp.split(pieces, piece_ends(pieces.shape[widest], count), axis=widest)  14.1 us
    transpose x1, local copies, waits for them, and re-layouts, own_block(): jnp.moveaxis(pieces, sequence, range(len(axes))).reshape(-1, *inside)  14.1 us
  transfers between devices with their start and end apart: 9, of which 7 were waited for; matrix products, arithmetic and copies ran while one was open for 6% of the time, Pallas kernels for 0%

profile of v1, /device:TPU:2, one launch (start us, length us, event | category | flops | bytes accessed | tf_op | source)
XLA Modules:
  0.0 567.5 jit_solution(6111918666446514028)
XLA Ops:
  7.2 1.1 copy.109
  8.3 5.1 stack.26
  13.3 11.7 %all-to-all-start = ((bf16[32,96,4,384]{3,1,2,0:T(8,128)(2,1)}), bf16[32,96,4,384]{3,1,2,0:T(8,128)(2,1)}, u32[]{:S(2)}, u32[]{:S(2)}) async-start(bf16[32,96,4,384]{3,1,2,0:T(8,128)(2,1)} %stack.26), calls=%async_computation | async-start | bytes 18874368 | tf_op jit(solution)/shard_map/all_to_all | solution.py:146
  26.6 212.3 %all-to-all-done = bf16[32,96,4,384]{3,1,2,0:T(8,128)(2,1)} async-done(((bf16[32,96,4,384]{3,1,2,0:T(8,128)(2,1)}), bf16[32,96,4,384]{3,1,2,0:T(8,128)(2,1)}, u32[]{:S(2)}, u32[]{:S(2)}) %all-to-all-start) | async-done | bytes 9437216 | tf_op jit(solution)/shard_map/all_to_all | solution.py:146
  238.9 8.5 %copy.110 = bf16[32,96,4,384]{3,1,0,2:T(8,128)(2,1)} copy(bf16[32,96,4,384]{3,1,2,0:T(8,128)(2,1)} %all-to-all-done) | data formatting | bytes 18874368 | tf_op jit(solution)/shard_map/all_to_all | solution.py:146
  247.4 6.5 %slice.317 = bf16[3072,3,384]{2,0,1:T(8,128)(2,1)} slice(bf16[3072,4,384]{2,0,1:T(8,128)(2,1)} %bitcast.151), slice={[0:3072], [0:3], [0:384]} | slice | bytes 14155776 | tf_op jit(solution)/shard_map/slice | solution.py:150
  254.0 10.3 %copy.111 = bf16[3072,3,384]{0,2,1:T(8,128)(2,1)} copy(bf16[3072,3,384]{2,0,1:T(8,128)(2,1)} %slice.317) | data formatting | bytes 14155776 | tf_op jit(solution)/shard_map/slice | solution.py:150
  264.3 5.4 convolution_convert_fusion.3
  269.8 1.3 collective-permute-start.1
  271.1 2.3 fusion.9
  273.6 6.7 %collective-permute-start = (bf16[2,128,384]{2,1,0:T(8,128)(2,1)S(1)}, bf16[2,128,384]{2,1,0:T(8,128)(2,1)S(1)}, u32[]{:S(2)}, u32[]{:S(2)}) collective-permute-start(bf16[2,128,384]{2,1,0:T(8,128)(2,1)S(1)} %pad_maximum_fusion.4), channel_id=1, source_target_pairs={{0,8},{8,16},{16,24},{24,32},{32,40},{40,48},{48,56},{56,64},{64,7... | collective-permute-start | bytes 589832 | tf_op jit(solution)/shard_map/ppermute | solution.py:22
  281.5 2.2 collective-permute-done
  285.3 1.0 fusion.32
  289.1 1.0 copy-done.2
  291.1 5.1 collective-permute-start.2
  296.2 1.5 collective-permute-start.3
  297.6 1.4 fusion.8
  299.2 2.0 fusion.2
  301.2 2.4 copy.145
  303.6 4.9 copy.146
  308.9 1.3 fusion.14
  310.3 4.9 fusion.1
  315.2 15.7 %concatenate.45 = bf16[32,96,3,384]{1,0,3,2:T(8,128)(2,1)} reshape(bf16[3072,1152]{0,1:T(8,128)(2,1)} %fusion.1) | data formatting | bytes 14155776 | tf_op jit(solution)/shard_map/concatenate | solution.py:184
  330.9 20.5 %slice_maximum_fusion = (bf16[32,48,4,384]{1,0,3,2:T(8,128)(2,1)}, bf16[8,4,48,4,384]{2,0,1,4,3:T(8,128)(2,1)}) fusion(bf16[32,96,1,384]{1,0,3,2:T(8,128)(2,1)} %copy.146, bf16[32,96,3,384]{1,0,3,2:T(8,128)(2,1)} %concatenate.45), kind=kLoop, calls=%fused_computation.2 | loop fusion | flops 18874368 | bytes 18874368 | tf_op jit(solution)/shard_map/concatenate | solution.py:184
  351.3 14.1 %copy.148 = bf16[8,4,48,4,384]{4,2,3,1,0:T(8,128)(2,1)} copy(bf16[8,4,48,4,384]{2,0,1,4,3:T(8,128)(2,1)} %get-tuple-element.121) | data formatting | bytes 9437184 | tf_op jit(solution)/shard_map/transpose | solution.py:44
  365.5 14.1 %copy.147 = bf16[32,48,4,384]{3,1,2,0:T(8,128)(2,1)} copy(bf16[32,48,4,384]{1,0,3,2:T(8,128)(2,1)} %get-tuple-element.120) | data formatting | bytes 9437184 | tf_op jit(solution)/shard_map/split | solution.py:55
  379.6 56.3 %reduce-scatter.9.cloned.1.call-done = bf16[4,48,4,384]{3,1,2,0:T(8,128)(2,1)} async-done(((bf16[32,48,4,384]{3,1,2,0:T(8,128)(2,1)}), bf16[4,48,4,384]{3,1,2,0:T(8,128)(2,1)}) %reduce-scatter.9.cloned.1.call-update) | async-done | bytes 589840 | tf_op jit(solution)/shard_map/reduce_scatter | solution.py:46
  436.0 54.8 %reduce-scatter.5.cloned.1.call-done = bf16[8,48,4,384]{3,1,2,0:T(8,128)(2,1)} async-done(((bf16[32,48,4,384]{3,1,2,0:T(8,128)(2,1)}), bf16[8,48,4,384]{3,1,2,0:T(8,128)(2,1)}) %reduce-scatter.5.cloned.1.call-update) | async-done | bytes 1179664 | tf_op jit(solution)/shard_map/reduce_scatter | solution.py:46
  490.8 4.3 convolution_convert_fusion.2
  495.2 16.3 %all_to_all.10 = bf16[8,128,384]{2,1,0:T(8,128)(2,1)S(1)} all-to-all(bf16[8,128,384]{2,1,0:T(8,128)(2,1)S(1)} %bitcast.160), channel_id=1, replica_groups=mesh['seq_0'=4,'seq_1'=8,'head'=8] {'head'}, dimensions={0} | all-to-all | bytes 1572864 | tf_op jit(solution)/shard_map/all_to_all | solution.py:65
  512.3 5.2 reduce-scatter.11.cloned.1.call-done
  517.5 41.6 %reduce-scatter.7.cloned.1.call-done = bf16[1,48,4,384]{3,1,2,0:T(8,128)(2,1)} async-done(((bf16[8,48,4,384]{3,1,2,0:T(8,128)(2,1)}), bf16[1,48,4,384]{3,1,2,0:T(8,128)(2,1)}) %reduce-scatter.7.cloned.1.call-update) | async-done | bytes 147472 | tf_op jit(solution)/shard_map/reduce_scatter | solution.py:46
  (79 shorter events, 11.5 us)
Async XLA Ops:
  7.2 257.1 %copy-start = (bf16[128,3072]{1,0:T(8,128)(2,1)S(1)}, bf16[128,3072]{1,0:T(8,128)(2,1)}, u32[]{:S(2)}) copy-start(bf16[128,3072]{1,0:T(8,128)(2,1)} %param.24) | copy-start | bytes 2359300
  13.3 11.8 %copy-start.8 = (s32[32]{0:T(128)S(1)}, s32[32]{0:T(128)}, u32[]{:S(2)}) copy-start(s32[32]{0:T(128)} %param.27) | copy-start | bytes 388
  13.3 225.6 %all-to-all-start = ((bf16[32,96,4,384]{3,1,2,0:T(8,128)(2,1)}), bf16[32,96,4,384]{3,1,2,0:T(8,128)(2,1)}, u32[]{:S(2)}, u32[]{:S(2)}) async-start(bf16[32,96,4,384]{3,1,2,0:T(8,128)(2,1)} %stack.26), calls=%async_computation | async-start | bytes 18874368 | tf_op jit(solution)/shard_map/all_to_all | solution.py:146
  25.1 410.8 %reduce-scatter.9.cloned.1.call-start = ((), (), s32[]{:S(2)}) async-start(), calls=%async_computation.8 | async-start | bytes 5308416 | tf_op jit(solution)/shard_map/reduce_scatter | solution.py:46
  264.3 6.8 %copy-start.3 = (bf16[128,3072]{1,0:T(8,128)(2,1)S(1)}, bf16[128,3072]{1,0:T(8,128)(2,1)}, u32[]{:S(2)}) copy-start(bf16[128,3072]{1,0:T(8,128)(2,1)} %param.25) | copy-start | bytes 2359300
  269.8 11.2 %collective-permute-start.1 = (bf16[2,128,384]{2,1,0:T(8,128)(2,1)S(1)}, bf16[2,128,384]{2,1,0:T(8,128)(2,1)S(1)}, u32[]{:S(2)}, u32[]{:S(2)}) collective-permute-start(bf16[2,128,384]{2,1,0:T(8,128)(2,1)S(1)} %pad_maximum_fusion.4), channel_id=1, source_target_pairs={{8,0},{16,8},{24,16},{32,24},{40,32},{48,40},{56,48},{64,56},{72,6... | collective-permute-start | bytes 589832 | tf_op jit(solution)/shard_map/ppermute | solution.py:24
  273.6 10.1 %collective-permute-start = (bf16[2,128,384]{2,1,0:T(8,128)(2,1)S(1)}, bf16[2,128,384]{2,1,0:T(8,128)(2,1)S(1)}, u32[]{:S(2)}, u32[]{:S(2)}) collective-permute-start(bf16[2,128,384]{2,1,0:T(8,128)(2,1)S(1)} %pad_maximum_fusion.4), channel_id=1, source_target_pairs={{0,8},{8,16},{16,24},{24,32},{32,40},{40,48},{48,56},{56,64},{64,7... | collective-permute-start | bytes 589832 | tf_op jit(solution)/shard_map/ppermute | solution.py:22
  280.6 6.1 %copy-start.4 = (bf16[1,1,128,3,128]{4,2,1,3,0:T(8,128)(2,1)}, bf16[1,1,128,3,128]{4,2,1,3,0:T(8,128)(2,1)S(1)}, u32[]{:S(2)}) copy-start(bf16[1,1,128,3,128]{4,2,1,3,0:T(8,128)(2,1)S(1)} %copy.116) | copy-start | bytes 294916
  281.3 5.4 copy-start.5
  284.0 2.7 copy-start.6
  286.7 0.7 copy-start.7
  289.1 1.0 copy-start.2
  291.1 17.5 %collective-permute-start.2 = (f32[2,128,384]{2,1,0:T(8,128)}, f32[2,128,384]{2,1,0:T(8,128)}, u32[]{:S(2)}, u32[]{:S(2)}) collective-permute-start(f32[2,128,384]{2,1,0:T(8,128)} %get-tuple-element.122), channel_id=1, source_target_pairs={{0,8},{8,16},{16,24},{24,32},{32,40},{40,48},{48,56},{56,64},{64,7... | collective-permute-start | bytes 1179656 | tf_op jit(solution)/shard_map/ppermute | solution.py:22
  296.2 12.8 %collective-permute-start.3 = (f32[2,128,384]{2,1,0:T(8,128)}, f32[2,128,384]{2,1,0:T(8,128)}, u32[]{:S(2)}, u32[]{:S(2)}) collective-permute-start(f32[2,128,384]{2,1,0:T(8,128)} %get-tuple-element.123), channel_id=1, source_target_pairs={{8,0},{16,8},{24,16},{32,24},{40,32},{48,40},{56,48},{64,56},{72,6... | collective-permute-start | bytes 1179656 | tf_op jit(solution)/shard_map/ppermute | solution.py:24
  365.4 125.4 %reduce-scatter.5.cloned.1.call-start = ((), (), s32[]{:S(2)}) async-start(), calls=%async_computation.6 | async-start | bytes 5898240 | tf_op jit(solution)/shard_map/reduce_scatter | solution.py:46
  379.6 138.0 %reduce-scatter.11.cloned.1.call-start = ((), (), s32[]{:S(2)}) async-start(), calls=%async_computation.9 | async-start | bytes 737280 | tf_op jit(solution)/shard_map/reduce_scatter | solution.py:46
  435.9 123.2 %reduce-scatter.7.cloned.1.call-start = ((), (), s32[]{:S(2)}) async-start(), calls=%async_computation.7 | async-start | bytes 1327104 | tf_op jit(solution)/shard_map/reduce_scatter | solution.py:46
  490.8 70.2 %copy-start.1 = (bf16[128,3072]{1,0:T(8,128)(2,1)S(1)}, bf16[128,3072]{1,0:T(8,128)(2,1)}, u32[]{:S(2)}) copy-start(bf16[128,3072]{1,0:T(8,128)(2,1)} %param.24) | copy-start | bytes 2359300
Sparse Core Ops, SparseCore 0:
  365.5 70.3 reduce-scatter.8
  438.4 52.3 reduce-scatter.4
  493.3 24.1 reduce-scatter.10
  519.9 39.1 reduce-scatter.6
